TPU v7x, 32 devices: a whole 2x2x4 slice. The times are simulated.
32 devices in a mesh: dp: 16 (over z, y, core), mp: 2 (over x).
Axes of the slice: x: 2, y: 2, z: 4, core: 2. Of those that a mesh axis runs over, the one named last changes fastest.
Arguments:
- patch_counts: int32 [128], P('dp'), may hold values from 100 to 240, as said below
- tokens: bfloat16 [128, 280, 768], P('dp'), may hold values from -6 to 6
- cotangent: bfloat16 [128, 280, 768], P('dp'), may hold values from -6 to 6
- attn_gain: float32 [768], P('dp'), may hold values from 0.1 to 1.9
- attn_shift: float32 [768], P('dp'), may hold values from -1.75 to 1.75
- w_qkv: float32 [768, 3, 768], P('dp', None, 'mp'), may hold values from -0.21875 to 0.21875
- b_qv: float32 [2, 768], P(None, 'mp'), may hold values from -3 to 3
- w_proj: float32 [768, 768], P('mp', 'dp'), may hold values from -0.875 to 0.875
- b_proj: float32 [768], P('dp'), may hold values from -3 to 3
- ffn_gain: float32 [768], P('dp'), may hold values from 0.1 to 1.9
- ffn_shift: float32 [768], P('dp'), may hold values from -1.75 to 1.75
- w_up: float32 [768, 3072], P('dp', 'mp'), may hold values from -0.21875 to 0.21875
- b_up: float32 [3072], P('mp'), may hold values from -3 to 3
- w_down: float32 [3072, 768], P('mp', 'dp'), may hold values from -0.109375 to 0.109375
- b_down: float32 [768], P('dp'), may hold values from -3 to 3
Outputs:
- block_out: bfloat16 [128, 280, 768], P('dp')
- tokens_grad: bfloat16 [128, 280, 768], P('dp')
- attn_gain_grad: float32 [768], P('dp')
- attn_shift_grad: float32 [768], P('dp')
- w_qkv_grad: float32 [768, 3, 768], P('dp', None, 'mp')
- b_qv_grad: float32 [2, 768], P(None, 'mp')
- w_proj_grad: float32 [768, 768], P('mp', 'dp')
- b_proj_grad: float32 [768], P('dp')
- ffn_gain_grad: float32 [768], P('dp')
- ffn_shift_grad: float32 [768], P('dp')
- w_up_grad: float32 [768, 3072], P('dp', 'mp')
- b_up_grad: float32 [3072], P('mp')
- w_down_grad: float32 [3072, 768], P('mp', 'dp')
- b_down_grad: float32 [768], P('dp')
Inputs may be any that keep to these rules, and one draw needn't show every extreme that they name: `patch_counts`: patch count of each pair; in every draw some pair has exactly 240 patches and some exactly 100.
All inputs are finite; a program needn't handle non-finite values.
Results may differ from a plain program's by a relative error of at most 0.022.
Values may be sent and summed in bfloat16 or wider, within the bound.
A program may use at most 192 MiB of HBM per device.

v0:
```python
import math
import jax
import jax.numpy as jnp
from jax import lax
from jax.sharding import PartitionSpec as P

HEADS = 12
HEAD_DIM = 64
TEXT = 40


def normalize(values, gain, shift):
    center = values - jnp.mean(values, axis=-1, keepdims=True)
    spread = jnp.mean(center * center, axis=-1, keepdims=True)
    return center * lax.rsqrt(spread + 1e-06) * gain + shift


def norm_back(values, gain, incoming):
    _, pullback = jax.vjp(lambda member, scaling: normalize(member, scaling, 0.0), values, gain)
    d_values, d_gain = pullback(incoming)
    return (d_values, d_gain, jnp.sum(incoming, axis=(0, 1)))


def per_device(
    patch_counts,
    tokens,
    cotangent,
    attn_gain,
    attn_shift,
    w_qkv,
    b_qv,
    w_proj,
    b_proj,
    ffn_gain,
    ffn_shift,
    w_up,
    b_up,
    w_down,
    b_down,
):
    low_type = jnp.bfloat16
    pair_count, rows_pair, _ = tokens.shape
    head_count = HEADS // lax.axis_size("mp")
    local_width = w_qkv.shape[2]
    score_scale = HEAD_DIM ** (-0.5)
    pair_block = math.gcd(pair_count, -(-512 // rows_pair))
    block_count = pair_count // pair_block
    gathered = (
        lax.all_gather(w_qkv.astype(low_type), "dp", axis=0, tiled=True),
        lax.all_gather(w_proj.astype(low_type), "dp", axis=1, tiled=True),
        lax.all_gather(w_up.astype(low_type), "dp", axis=0, tiled=True),
        lax.all_gather(w_down.astype(low_type), "dp", axis=1, tiled=True),
        lax.all_gather(attn_gain.astype(low_type), "dp", axis=0, tiled=True),
        lax.all_gather(attn_shift.astype(low_type), "dp", axis=0, tiled=True),
        lax.all_gather(b_proj.astype(low_type), "dp", axis=0, tiled=True),
        lax.all_gather(ffn_gain.astype(low_type), "dp", axis=0, tiled=True),
        lax.all_gather(ffn_shift.astype(low_type), "dp", axis=0, tiled=True),
        lax.all_gather(b_down.astype(low_type), "dp", axis=0, tiled=True),
    )
    qkv_full, proj_full, up_full, down_full = (gathered[0], gathered[1], gathered[2], gathered[3])
    gain_one = gathered[4].astype(jnp.float32)
    shift_one = gathered[5].astype(jnp.float32)
    proj_bias = gathered[6].astype(jnp.float32)
    gain_two = gathered[7].astype(jnp.float32)
    shift_two = gathered[8].astype(jnp.float32)
    down_bias = gathered[9].astype(jnp.float32)
    bias_qv = b_qv.astype(low_type).astype(jnp.float32)
    up_bias = b_up.astype(low_type).astype(jnp.float32)
    row_valid = (
        jnp.arange(rows_pair, dtype=jnp.int32)[None, :] < (TEXT + patch_counts)[:, None]
    ).astype(jnp.float32)
    inputs = tokens.astype(jnp.float32)
    normed_one = normalize(inputs, gain_one, shift_one).astype(low_type)
    qkv = jnp.einsum("psd,dtc->pstc", normed_one, qkv_full, preferred_element_type=jnp.float32)
    queries = (qkv[:, :, 0] + bias_qv[0]).astype(low_type)
    key_rows = qkv[:, :, 1].astype(low_type)
    values = (qkv[:, :, 2] + bias_qv[1]).astype(low_type)

    def by_blocks(array):
        return array.reshape(block_count, pair_block, rows_pair, head_count, HEAD_DIM)

    key_mask = row_valid.reshape(block_count, pair_block, rows_pair)

    def score_rows(query_block, key_block, mask_block):
        raw = (
            jnp.einsum(
                "bqhe,bkhe->bhqk", query_block, key_block, preferred_element_type=jnp.float32
            )
            * score_scale
        )
        return jnp.where(mask_block[:, None, None, :] > 0, raw, -1e30)

    def attend(operands):
        query_block, key_block, value_block, mask_block = operands
        scores = score_rows(query_block, key_block, mask_block)
        row_max = jnp.max(scores, axis=-1, keepdims=True)
        expo = jnp.exp(scores - row_max)
        row_total = jnp.sum(expo, axis=-1, keepdims=True)
        probabilities = (expo / row_total).astype(low_type)
        attended_block = jnp.einsum(
            "bhqk,bkhe->bqhe", probabilities, value_block, preferred_element_type=jnp.float32
        ).astype(low_type)
        log_total = row_max[..., 0] + jnp.log(row_total[..., 0])
        return (attended_block, log_total)

    attended_blocks, log_totals = lax.map(
        attend, (by_blocks(queries), by_blocks(key_rows), by_blocks(values), key_mask)
    )
    attended = attended_blocks.reshape(pair_count, rows_pair, local_width)
    proj_part = jnp.einsum("psc,cd->psd", attended, proj_full, preferred_element_type=jnp.float32)
    attn_sum = lax.psum(proj_part.astype(jnp.bfloat16), "mp").astype(jnp.float32)
    hidden = inputs + attn_sum + proj_bias
    normed_two = normalize(hidden, gain_two, shift_two).astype(low_type)
    pre_act = (
        jnp.einsum("psd,df->psf", normed_two, up_full, preferred_element_type=jnp.float32) + up_bias
    )
    active = jax.nn.gelu(pre_act, approximate=False).astype(low_type)
    down_part = jnp.einsum("psf,fd->psd", active, down_full, preferred_element_type=jnp.float32)
    mlp_sum = lax.psum(down_part.astype(jnp.bfloat16), "mp").astype(jnp.float32)
    block_out = ((hidden + mlp_sum + down_bias) * row_valid[:, :, None]).astype(low_type)
    qkv_back, proj_back, up_back, down_back = (qkv_full, proj_full, up_full, down_full)
    gain_one_back, gain_two_back = (gain_one, gain_two)
    upstream = cotangent.astype(jnp.float32) * row_valid[:, :, None]
    upstream_low = upstream.astype(low_type)
    grad_b_down = jnp.sum(upstream, axis=(0, 1))
    grad_w_down = jnp.einsum(
        "psf,psd->fd", active, upstream_low, preferred_element_type=jnp.float32
    )
    d_active = jnp.einsum(
        "psd,fd->psf", upstream_low, down_back, preferred_element_type=jnp.float32
    )
    _, gelu_pull = jax.vjp(lambda member: jax.nn.gelu(member, approximate=False), pre_act)
    d_pre = gelu_pull(d_active)[0].astype(low_type)
    grad_b_up = jnp.sum(d_pre, axis=(0, 1), dtype=jnp.float32)
    grad_w_up = jnp.einsum("psd,psf->df", normed_two, d_pre, preferred_element_type=jnp.float32)
    d_normed_two = lax.psum(
        jnp.einsum("psf,df->psd", d_pre, up_back, preferred_element_type=jnp.float32).astype(
            jnp.bfloat16
        ),
        "mp",
    ).astype(jnp.float32)
    d_hidden_norm, grad_gain_two, grad_shift_two = norm_back(hidden, gain_two_back, d_normed_two)
    d_hidden = upstream + d_hidden_norm
    grad_b_proj = jnp.sum(d_hidden, axis=(0, 1))
    d_hidden_low = d_hidden.astype(low_type)
    grad_w_proj = jnp.einsum(
        "psc,psd->cd", attended, d_hidden_low, preferred_element_type=jnp.float32
    )
    d_attended = jnp.einsum(
        "psd,cd->psc", d_hidden_low, proj_back, preferred_element_type=jnp.float32
    ).astype(low_type)

    def attend_back(operands):
        query_block, key_block, value_block, mask_block, log_total, d_out = operands
        scores = score_rows(query_block, key_block, mask_block)
        probabilities = jnp.exp(scores - log_total[..., None])
        d_probs = jnp.einsum(
            "bqhe,bkhe->bhqk", d_out, value_block, preferred_element_type=jnp.float32
        )
        d_value = jnp.einsum(
            "bhqk,bqhe->bkhe",
            probabilities.astype(low_type),
            d_out,
            preferred_element_type=jnp.float32,
        )
        inner = jnp.sum(probabilities * d_probs, axis=-1, keepdims=True)
        d_scores = (probabilities * (d_probs - inner)).astype(low_type)
        d_query = score_scale * jnp.einsum(
            "bhqk,bkhe->bqhe", d_scores, key_block, preferred_element_type=jnp.float32
        )
        d_key = score_scale * jnp.einsum(
            "bhqk,bqhe->bkhe", d_scores, query_block, preferred_element_type=jnp.float32
        )
        return jnp.stack([d_query, d_key, d_value], axis=2).astype(low_type)

    d_blocks = lax.map(
        attend_back,
        (
            by_blocks(queries),
            by_blocks(key_rows),
            by_blocks(values),
            key_mask,
            log_totals,
            by_blocks(d_attended),
        ),
    )
    d_qkv = d_blocks.reshape(pair_count, rows_pair, 3, local_width)
    column_sums = jnp.sum(d_qkv, axis=(0, 1), dtype=jnp.float32)
    grad_b_qv = jnp.stack([column_sums[0], column_sums[2]], axis=0)
    grad_w_qkv = jnp.einsum("psd,pstc->dtc", normed_one, d_qkv, preferred_element_type=jnp.float32)
    d_normed_one = lax.psum(
        jnp.einsum("pstc,dtc->psd", d_qkv, qkv_back, preferred_element_type=jnp.float32).astype(
            jnp.bfloat16
        ),
        "mp",
    ).astype(jnp.float32)
    d_input_norm, grad_gain_one, grad_shift_one = norm_back(inputs, gain_one_back, d_normed_one)
    tokens_grad = (d_hidden + d_input_norm).astype(low_type)
    bias_grads = lax.psum((grad_b_qv, grad_b_up), "dp")
    summed = (
        lax.psum_scatter(grad_w_qkv, "dp", scatter_dimension=0, tiled=True),
        lax.psum_scatter(grad_w_proj, "dp", scatter_dimension=1, tiled=True),
        lax.psum_scatter(grad_w_up, "dp", scatter_dimension=0, tiled=True),
        lax.psum_scatter(grad_w_down, "dp", scatter_dimension=1, tiled=True),
        lax.psum_scatter(grad_gain_one, "dp", scatter_dimension=0, tiled=True),
        lax.psum_scatter(grad_shift_one, "dp", scatter_dimension=0, tiled=True),
        lax.psum_scatter(grad_b_proj, "dp", scatter_dimension=0, tiled=True),
        lax.psum_scatter(grad_gain_two, "dp", scatter_dimension=0, tiled=True),
        lax.psum_scatter(grad_shift_two, "dp", scatter_dimension=0, tiled=True),
        lax.psum_scatter(grad_b_down, "dp", scatter_dimension=0, tiled=True),
    )
    out_qkv, out_proj, out_up, out_down = (summed[0], summed[1], summed[2], summed[3])
    out_gain_one, out_shift_one, out_bproj = (summed[4], summed[5], summed[6])
    out_gain_two, out_shift_two, out_bdown = (summed[7], summed[8], summed[9])
    return (
        block_out,
        tokens_grad,
        out_gain_one,
        out_shift_one,
        out_qkv,
        bias_grads[0],
        out_proj,
        out_bproj,
        out_gain_two,
        out_shift_two,
        out_up,
        bias_grads[1],
        out_down,
        out_bdown,
    )


def solution(mesh):
    in_specs = (
        P("dp"),
        P("dp", None, None),
        P("dp", None, None),
        P("dp"),
        P("dp"),
        P("dp", None, "mp"),
        P(None, "mp"),
        P("mp", "dp"),
        P("dp"),
        P("dp"),
        P("dp"),
        P("dp", "mp"),
        P("mp"),
        P("mp", "dp"),
        P("dp"),
    )
    out_specs = (
        P("dp", None, None),
        P("dp", None, None),
        P("dp"),
        P("dp"),
        P("dp", None, "mp"),
        P(None, "mp"),
        P("mp", "dp"),
        P("dp"),
        P("dp"),
        P("dp"),
        P("dp", "mp"),
        P("mp"),
        P("mp", "dp"),
        P("dp"),
    )
    return jax.shard_map(
        per_device, mesh=mesh, in_specs=in_specs, out_specs=out_specs, check_vma=False
    )
```

profile of v0, /device:TPU:0, one launch (start us, length us, event | category | flops | bytes accessed | tf_op | source)
XLA Modules:
  0.0 1070.2 jit_solution(13060933296893398383)
XLA Ops:
  20.8 63.2 %all-reduce.13 = (bf16[768]{0:T(1024)(128)(2,1)}, bf16[768]{0:T(1024)(128)(2,1)}, bf16[768]{0:T(1024)(128)(2,1)}, bf16[768]{0:T(1024)(128)(2,1)}, bf16[768]{0:T(1024)(128)(2,1)}, /*index=5*/bf16[768]{0:T(1024)(128)(2,1)}) all-reduce(bf16[768]{0:T(1024)(128)(2,1)} %dynamic-update-slice.4, ...), channel_id=1, replica_groups=mesh['dp'=16,'mp'=2] {'dp'}, use_global_device_ids=true, to_apply=%add.4 | all-reduce | flops 4608 | bytes 18432
  97.2 20.3 %all_gather.33 = bf16[384,768]{0,1:T(8,128)(2,1)} all-gather(bf16[384,48]{0,1:T(8,128)(2,1)S(1)} %convert_element_type.183), channel_id=1, replica_groups=mesh['dp'=16,'mp'=2] {'dp'}, dimensions={1}, use_global_device_ids=true | all-gather | bytes 626688 | tf_op jit(solution)/shard_map/all_gather | solution.py:50
  144.8 7.3 add_convert_fusion.3
  152.2 32.6 %while.22 = (s32[]{:T(128)}, bf16[4,2,280,6,64]{2,4,3,1,0:T(8,128)(2,1)}, f32[4,2,6,280]{3,2,1,0:T(8,128)S(1)}, bf16[4,2,280,6,64]{2,4,3,1,0:T(8,128)(2,1)}, f32...) while((s32[]{:T(128)}, ...), condition=%wide.region_5.6_spmd, body=%wide.region_2.5_spmd.sunk | while | flops 252346640 | bytes 13796445 | solution.py:106
  198.1 83.8 %all-reduce.19.cloned.1.call-done = bf16[8,280,768]{2,1,0:T(8,128)(2,1)} async-done(((bf16[8,280,768]{2,1,0:T(8,128)(2,1)}), bf16[8,280,768]{2,1,0:T(8,128)(2,1)}) %all-reduce.19.cloned.1.call-update) | async-done | bytes 3440656 | tf_op jit(solution)/shard_map/psum | solution.py:111
  288.5 38.6 %all-gather.6.cloned.1.call-done = bf16[768,1536]{1,0:T(8,128)(2,1)} async-done(((bf16[48,1536]{1,0:T(8,128)(2,1)}), bf16[768,1536]{1,0:T(8,128)(2,1)}) %all-gather.6.cloned.1.call-update) | async-done | bytes 2359312 | tf_op jit(solution)/shard_map/all_gather | solution.py:51
  327.1 13.9 %fusion.86 = (u8[280,1536]{1,0:T(8,128)(4,1)S(1)}, u8[280,1536]{1,0:T(8,128)(4,1)S(1)}, f32[8,280,1536]{2,1,0:T(8,128)S(1)}) fusion(f32[1536]{0:T(1024)} %convert_convert_fusion, bf16[768,1536]{1,0:T(8,128)(2,1)} %all-gather.6.cloned.1.call-done, f32[768]{0:T(1024)} %convert_element_type.191, f32[768]{0:T(1024)} %convert_element_type.189, ...), kind=kOutput, calls=%fused_computation.134 | convolution fusion | flops 5347614720 | bytes 23896576 | tf_op jit(solution)/shard_map/psd,df->psf/dot_general | solution.py:115
  346.0 32.9 %multiply_convert_fusion.1 = (bf16[8,280,1536]{2,1,0:T(8,128)(2,1)}, f32[8,280,1536]{2,1,0:T(8,128)}) fusion(f32[8,280,1536]{2,1,0:T(8,128)S(1)} %get-tuple-element.187, f32[1536]{0:T(1024)S(1)} %copy-done.25, u8[280,1536]{1,0:T(8,128)(4,1)S(1)} %get-tuple-element.113, u8[280,1536]{1,0:T(8,128)(4,1)S(1)} %get-tuple-element.112), kind=kLoop, calls=%fused_computation.75 | loop fusion | flops 244285440 | bytes 35272704 | tf_op jit(solution)/shard_map/convert_element_type | solution.py:117
  378.9 18.8 %convert_reduce_fusion.1 = (f32[1536]{0:T(1024)}, bf16[8,280,1536]{2,1,0:T(8,128)(2,1)}) fusion(f32[8,280,1536]{2,1,0:T(8,128)} %get-tuple-element.173, bf16[1536,768]{0,1:T(8,128)(2,1)} %all-gather.8.cloned.1.call-done, bf16[8,280,768]{2,1,0:T(8,128)(2,1)} %param.21, f32[8,280]{1,0:T(8,128)} %fusion.108, f32[8,280,1536]{2,1,0:T(8,128)} %copy-done.6, ...), kind=kOutput, calls=%fused_computation.73 | convolution fusion | flops 5348473344 | bytes 40227584 | tf_op jit(solution)/shard_map/psd,fd->psf/dot_general | solution.py:129
  397.6 10.0 convolution_convert_fusion
  407.7 10.0 convolution_convert_fusion.1
  417.7 81.1 %all-reduce.21.cloned.1.call-done = bf16[8,280,768]{2,1,0:T(8,128)(2,1)} async-done(((bf16[8,280,768]{2,1,0:T(8,128)(2,1)}), bf16[8,280,768]{2,1,0:T(8,128)(2,1)}) %all-reduce.21.cloned.1.call-update) | async-done | bytes 3440656 | tf_op jit(solution)/shard_map/psum | solution.py:136
  525.6 64.1 %while.23 = (s32[]{:T(128)}, bf16[4,2,280,3,6,64]{2,5,4,1,3,0:T(8,128)(2,1)}, bf16[4,2,280,6,64]{2,4,3,1,0:T(8,128)(2,1)}, f32[4,2,280]{2,1,0:T(2,128)}, bf16[4,...) while((s32[]{:T(128)}, ...), condition=%wide.region_15.16_spmd, body=%wide.region_13.15_spmd.sunk | while | flops 621167104 | bytes 36805476 | solution.py:176
  596.9 7.7 bitcast_convert_fusion
  604.8 7.4 fusion.101
  612.3 12.6 %convolution_bitcast_fusion.1 = f32[768,1536]{1,0:T(8,128)} fusion(bf16[8,280,1536]{2,1,0:T(8,128)(2,1)} %get-tuple-element.189, f32[768]{0:T(1024)S(1)} %copy-done.35, f32[768]{0:T(1024)S(1)} %copy-done.24, f32[8,280]{1,0:T(8,128)S(1)} %copy-done.20, f32[8,280]{1,0:T(8,128)S(1)} %broadcast_multiply_fusion, f32[768]{0:T(1024)S(1)} %convert_element_type.187, ...), kind=kOutput, calls=%fused_computation.130 | convolution fusion | flops 5300305920 | bytes 18508288 | tf_op jit(solution)/shard_map/psd,psf->df/dot_general | solution.py:135
  625.0 11.0 %convolution_bitcast_fusion = f32[1536,768]{0,1:T(8,128)} fusion(bf16[8,280,1536]{2,1,0:T(8,128)(2,1)} %get-tuple-element.172, bf16[8,280,768]{2,1,0:T(8,128)(2,1)} %param.21, f32[8,280]{1,0:T(8,128)S(1)} %copy-done.18), kind=kOutput, calls=%fused_computation.129 | convolution fusion | flops 5289984000 | bytes 15049472 | tf_op jit(solution)/shard_map/psf,psd->fd/dot_general | solution.py:126
  636.3 13.7 %convolution_bitcast_fusion.2 = f32[768,3,384]{2,0,1:T(8,128)} fusion(bf16[8,280,3,384]{1,3,2,0:T(8,128)(2,1)} %bitcast.170, bf16[8,280,768]{2,1,0:T(8,128)(2,1)S(1)} %copy-done, f32[768]{0:T(1024)S(1)} %copy-done.34, f32[768]{0:T(1024)S(1)} %copy-done.22, f32[8,280]{1,0:T(8,128)S(1)} %copy-done.16, f32[8,280]{1,0:T(8,128)S(1)} %copy-done.11), kind=kOutput, calls=%fused_computation.144 | convolution fusion | flops 3973939200 | bytes 12164608 | tf_op jit(solution)/shard_map/psd,pstc->dtc/dot_general | solution.py:190
  655.3 115.5 %all-reduce.23.cloned.1.call-done = (bf16[8,280,768]{2,1,0:T(8,128)(2,1)}, bf16[8,280,768]{2,1,0:T(8,128)(2,1)}) async-done(((bf16[8,280,768]{2,1,0:T(8,128)(2,1)}, bf16[8,280,768]{2,1,0:T(8,128)(2,1)}), (bf16[8,280,768]{2,1,0:T(8,128)(2,1)}, bf16[8,280,768]{2,1,0:T(8,128)(2,1)})) %all-reduce.23.cloned.1.call-update) | async-done | bytes 6881296 | tf_op jit(solution)/shard_map/psum | solution.py:119
  779.3 61.8 %all-reduce.12 = (f32[768]{0:T(1024)S(1)}, f32[768]{0:T(1024)S(1)}, f32[2,384]{1,0:T(2,128)}, f32[768]{0:T(1024)}, f32[768]{0:T(1024)}, /*index=5*/f32[768]{0:T(1024)}, f32[1536]{0:T(1024)}, f32[768]{0:T(1024)S(1)}) all-reduce(f32[768]{0:T(1024)S(1)} %get-tuple-element.116, ...), channel_id=2, replica_groups=mesh['dp'=16,'mp'=2] {'dp'}, use_global_device_ids=true, to_apply=%region_20.21.clone | all-reduce | flops 6912 | bytes 55296
  846.6 11.0 %add_convert_fusion.1 = (bf16[8,280,768]{2,1,0:T(8,128)(2,1)}, bf16[8,280,768]{2,1,0:T(8,128)(2,1)}) fusion(f32[8,280,768]{2,1,0:T(8,128)} %copy-done.3, bf16[8,280,768]{2,1,0:T(8,128)(2,1)S(1)} %copy-done, bf16[8,280,768]{2,1,0:T(8,128)(2,1)} %get-tuple-element.169, f32[8,280]{1,0:T(8,128)S(1)} %negate_multiply_fusion.1, ...), kind=kLoop, calls=%fused_computation.116 | loop fusion | flops 32686080 | bytes 27579136 | tf_op jit(solution)/shard_map/convert_element_type | solution.py:198
  857.6 54.7 %reduce-scatter.9.cloned.1.call-done = f32[48,1536]{1,0:T(8,128)} async-done(((f32[768,1536]{1,0:T(8,128)}), f32[48,1536]{1,0:T(8,128)}) %reduce-scatter.9.cloned.1.call-update) | async-done | bytes 294928 | tf_op jit(solution)/shard_map/reduce_scatter | solution.py:203
  912.3 79.2 %reduce-scatter.11.cloned.1.call-done = f32[1536,48]{0,1:T(8,128)} async-done(((f32[1536,768]{0,1:T(8,128)}), f32[1536,48]{0,1:T(8,128)}) %reduce-scatter.11.cloned.1.call-update) | async-done | bytes 294928 | tf_op jit(solution)/shard_map/reduce_scatter | solution.py:204
  991.5 71.6 %reduce-scatter.5.cloned.1.call-done = f32[48,3,384]{2,0,1:T(8,128)} async-done(((f32[768,3,384]{2,0,1:T(8,128)}), f32[48,3,384]{2,0,1:T(8,128)}) %reduce-scatter.5.cloned.1.call-update) | async-done | bytes 221200 | tf_op jit(solution)/shard_map/reduce_scatter | solution.py:201
  (242 shorter events, 227.4 us)
Async XLA Ops:
  7.2 110.4 %copy-start = (bf16[8,280,768]{2,1,0:T(8,128)(2,1)S(1)}, bf16[8,280,768]{2,1,0:T(8,128)(2,1)}, u32[]{:S(2)}) copy-start(bf16[8,280,768]{2,1,0:T(8,128)(2,1)} %param.20) | copy-start | bytes 10321924
  7.2 110.3 %all-gather.4.cloned.1.call-start = ((), (), s32[]{:S(2)}) async-start(), calls=%async_computation.4 | async-start | bytes 1880064 | tf_op jit(solution)/shard_map/all_gather | solution.py:49
  9.0 272.9 %all-reduce.19.cloned.1.call-start = ((), (), s32[]{:S(2)}) async-start(), calls=%async_computation.5 | async-start | bytes 6881280 | tf_op jit(solution)/shard_map/psum | solution.py:111
  84.7 39.9 %copy-start.21 = (f32[768]{0:T(1024)}, f32[768]{0:T(1024)S(1)}, u32[]{:S(2)}) copy-start(f32[768]{0:T(1024)S(1)} %convert_element_type.172) | copy-start | bytes 9220
  92.9 31.7 %copy-start.10 = (f32[8,280]{1,0:T(8,128)}, f32[8,280]{1,0:T(8,128)S(1)}, u32[]{:S(2)}) copy-start(f32[8,280]{1,0:T(8,128)S(1)} %broadcast_multiply_fusion.1) | copy-start | bytes 26884
  184.8 12.1 %copy-start.37 = (bf16[768]{0:T(1024)(128)(2,1)S(1)}, bf16[768]{0:T(1024)(128)(2,1)}, u32[]{:S(2)}) copy-start(bf16[768]{0:T(1024)(128)(2,1)} %get-tuple-element.162) | copy-start | bytes 4612
  184.8 12.7 %copy-start.32 = (f32[1536]{0:T(1024)S(1)}, f32[1536]{0:T(1024)}, u32[]{:S(2)}) copy-start(f32[1536]{0:T(1024)} %param.31) | copy-start | bytes 18436
  190.8 136.3 %all-gather.6.cloned.1.call-start = ((), (), s32[]{:S(2)}) async-start(), calls=%async_computation.6 | async-start | bytes 2506752 | tf_op jit(solution)/shard_map/all_gather | solution.py:51
  192.5 186.3 %all-gather.8.cloned.1.call-start = ((), (), s32[]{:S(2)}) async-start(), calls=%async_computation.7 | async-start | bytes 2506752 | tf_op jit(solution)/shard_map/all_gather | solution.py:52
  194.2 304.6 %all-reduce.21.cloned.1.call-start = ((), (), s32[]{:S(2)}) async-start(), calls=%async_computation.8 | async-start | bytes 6881280 | tf_op jit(solution)/shard_map/psum | solution.py:136
  327.1 18.9 %copy-start.25 = (f32[1536]{0:T(1024)S(1)}, f32[1536]{0:T(1024)}, u32[]{:S(2)}) copy-start(f32[1536]{0:T(1024)} %convert_convert_fusion) | copy-start | bytes 18436
  378.9 18.8 %copy-start.40 = (bf16[768,1536]{1,0:T(8,128)(2,1)S(1)}, bf16[768,1536]{1,0:T(8,128)(2,1)}, u32[]{:S(2)}) copy-start(bf16[768,1536]{1,0:T(8,128)(2,1)} %all-gather.6.cloned.1.call-done) | copy-start | bytes 7077892
  407.7 363.0 %all-reduce.23.cloned.1.call-start = ((), (), s32[]{:S(2)}) async-start(), calls=%async_computation.13 | async-start | bytes 13762560 | tf_op jit(solution)/shard_map/psum | solution.py:119
  604.6 253.0 %reduce-scatter.7.cloned.1.call-start = ((), (), s32[]{:S(2)}) async-start(), calls=%async_computation.10 | async-start | bytes 1253376 | tf_op jit(solution)/shard_map/reduce_scatter | solution.py:202
  612.2 12.8 %copy-start.18 = (f32[8,280]{1,0:T(8,128)S(1)}, f32[8,280]{1,0:T(8,128)}, u32[]{:S(2)}) copy-start(f32[8,280]{1,0:T(8,128)} %fusion.108) | copy-start | bytes 26884
  612.2 300.1 %reduce-scatter.9.cloned.1.call-start = ((), (), s32[]{:S(2)}) async-start(), calls=%async_computation.11 | async-start | bytes 5013504 | tf_op jit(solution)/shard_map/reduce_scatter | solution.py:203
  624.9 11.4 %copy-start.11 = (f32[8,280]{1,0:T(8,128)S(1)}, f32[8,280]{1,0:T(8,128)}, u32[]{:S(2)}) copy-start(f32[8,280]{1,0:T(8,128)} %copy-done.10) | copy-start | bytes 26884
  624.9 11.4 %copy-start.16 = (f32[8,280]{1,0:T(8,128)S(1)}, f32[8,280]{1,0:T(8,128)}, u32[]{:S(2)}) copy-start(f32[8,280]{1,0:T(8,128)} %fusion.109) | copy-start | bytes 26884
  624.9 11.4 %copy-start.22 = (f32[768]{0:T(1024)S(1)}, f32[768]{0:T(1024)}, u32[]{:S(2)}) copy-start(f32[768]{0:T(1024)} %copy-done.21) | copy-start | bytes 9220
  624.9 11.4 %copy-start.34 = (f32[768]{0:T(1024)S(1)}, f32[768]{0:T(1024)}, u32[]{:S(2)}) copy-start(f32[768]{0:T(1024)} %convert_element_type.174) | copy-start | bytes 9220
  624.9 366.6 %reduce-scatter.11.cloned.1.call-start = ((), (), s32[]{:S(2)}) async-start(), calls=%async_computation.12 | async-start | bytes 5013504 | tf_op jit(solution)/shard_map/reduce_scatter | solution.py:204
  636.0 14.1 %copy-start.36 = (bf16[768]{0:T(1024)(128)(2,1)S(1)}, bf16[768]{0:T(1024)(128)(2,1)}, u32[]{:S(2)}) copy-start(bf16[768]{0:T(1024)(128)(2,1)} %get-tuple-element.167) | copy-start | bytes 4612
  636.0 427.1 %reduce-scatter.5.cloned.1.call-start = ((), (), s32[]{:S(2)}) async-start(), calls=%async_computation.9 | async-start | bytes 3760128 | tf_op jit(solution)/shard_map/reduce_scatter | solution.py:201
  650.7 124.2 %copy-start.13 = (f32[8,280]{1,0:T(8,128)S(1)}, f32[8,280]{1,0:T(8,128)}, u32[]{:S(2)}) copy-start(f32[8,280]{1,0:T(8,128)} %copy-done.12) | copy-start | bytes 26884
  (28 other events, 165.5 us)
Sparse Core Ops, SparseCore 0:
  10.9 43.1 all-gather.3
  190.9 90.9 all-reduce.18
  284.8 42.3 all-gather.5
  329.8 41.0 all-gather.7
  407.8 90.9 all-reduce.20
  604.7 165.9 all-reduce.22
  774.9 58.1 reduce-scatter.6
  837.6 74.6 reduce-scatter.8
  916.7 74.7 reduce-scatter.10
  995.8 67.3 reduce-scatter.4
where the time goes:
time: 1080 us; the launch traced here: 1070 us
  waiting for transfers between devices  525 us (49%)
  matrix products  194 us (18%)
  blocking collectives  145 us (13%)
  other arithmetic  136 us (13%)
  local copies, waits for them, and re-layouts  53.1 us (5%)
  between operations  16.2 us (2%)
    unnamed x2, blocking collectives  125 us
    psum x1, waiting for transfers between devices, per_device(): mlp_sum = lax.psum(down_part.astype(jnp.bfloat16), 'mp').astype(jnp.float32)  115 us
    psum x1, waiting for transfers between devices, per_device(): lax.psum(proj_part.astype(jnp.bfloat16), 'mp').astype(jnp.float32)  83.8 us
    psum x1, waiting for transfers between devices, per_device(): lax.psum(jnp.einsum('psf,df->psd', d_pre, up_back, preferred_element_type...  81.1 us
    reduce_scatter x1, waiting for transfers between devices, per_device(): lax.psum_scatter(grad_w_down, 'dp', scatter_dimension=1, tiled=True)  79.2 us
    reduce_scatter x1, waiting for transfers between devices, per_device(): lax.psum_scatter(grad_w_qkv, 'dp', scatter_dimension=0, tiled=True)  71.6 us
    reduce_scatter x1, waiting for transfers between devices, per_device(): lax.psum_scatter(grad_w_up, 'dp', scatter_dimension=0, tiled=True)  54.7 us
    all_gather x1, waiting for transfers between devices, per_device(): lax.all_gather(w_up.astype(low_type), 'dp', axis=0, tiled=True)  38.6 us
  transfers between devices with their start and end apart: 10, of which 7 were waited for; matrix products, arithmetic and copies ran while one was open for 16% of the time, Pallas kernels for 0%

commit v1 on v0

--- a/solution.py
+++ b/solution.py
@@ -1,3 +1,4 @@
+import functools
 import math
 import jax
 import jax.numpy as jnp
@@ -7,6 +8,37 @@
 HEADS = 12
 HEAD_DIM = 64
 TEXT = 40
+
+
+def shape_loops_on(x0, group_axis, k_dim):
+    arr_out = jax.lax.axis_size(group_axis)
+    formed = jax.lax.axis_index(group_axis)
+    moved, main, answer = (arr_out, formed, x0.shape[k_dim])
+    part_now = jnp.zeros(
+        [p * moved if no == k_dim else p for no, p in enumerate(x0.shape)], x0.dtype
+    )
+    mixed_arr = r2 = x0
+    h_now = lax.dynamic_update_slice_in_dim(part_now, x0, main * answer, axis=k_dim)
+    for dev_j in range(1, moved // 2 + 1):
+        far_arr = range(moved)
+        r_now = map(lambda no: (no, (no + 1) % moved), far_arr)
+        base_arr = list(r_now)
+        mixed_arr = jax.lax.ppermute(mixed_arr, axis_name=group_axis, perm=base_arr)
+        h_now = lax.dynamic_update_slice_in_dim(
+            h_now, mixed_arr, (main - dev_j) % moved * answer, axis=k_dim
+        )
+        if 2 * dev_j < moved:
+            raw_out = range(moved)
+            later = map(lambda no: (no, (no - 1) % moved), raw_out)
+            a_now = list(later)
+            r2 = jax.lax.ppermute(r2, group_axis, perm=a_now)
+            h_now = lax.dynamic_update_slice_in_dim(
+                h_now, r2, (main + dev_j) % moved * answer, axis=k_dim
+            )
+    return h_now
+
+
+_proceed_cycles = functools.partial(shape_loops_on, group_axis="dp", k_dim=0)
 
 
 def normalize(values, gain, shift):
@@ -48,7 +80,7 @@
     gathered = (
         lax.all_gather(w_qkv.astype(low_type), "dp", axis=0, tiled=True),
         lax.all_gather(w_proj.astype(low_type), "dp", axis=1, tiled=True),
-        lax.all_gather(w_up.astype(low_type), "dp", axis=0, tiled=True),
+        _proceed_cycles(w_up.astype(low_type)),
         lax.all_gather(w_down.astype(low_type), "dp", axis=1, tiled=True),
         lax.all_gather(attn_gain.astype(low_type), "dp", axis=0, tiled=True),
         lax.all_gather(attn_shift.astype(low_type), "dp", axis=0, tiled=True),

time: 1080 us -> 1040 us (0.963)
  waiting for transfers between devices: 525 us -> 442 us
  starting transfers between devices: 0.8 us -> 32.2 us
  local copies, waits for them, and re-layouts: 53.1 us -> 66.3 us
    psum x1, waiting for transfers between devices: 83.8 us -> 24.4 us  [per_device(): lax.psum(proj_part.astype(jnp.bfloat16), 'mp').astype(jnp.float32)]
    all_gather x1 -> x0, waiting for transfers between devices: 38.6 us -> none  [per_device(): lax.all_gather(w_up.astype(low_type), 'dp', axis=0, tiled=True)]
    ppermute x0 -> x15, starting transfers between devices: none -> 31.3 us  [the longest x7 30.7 us: shape_loops_on(): r2 = jax.lax.ppermute(r2, group_axis, perm=a_now)]
    ppermute x0 -> x15, waiting for transfers between devices: none -> 13.7 us  [the longest x8 13.7 us: shape_loops_on(): mixed_arr = jax.lax.ppermute(mixed_arr, axis_name=group_axis, perm=base_arr)]
    dynamic_update_slice x0 -> x15, local copies, waits for them, and re-layouts: none -> 11.9 us  [the longest x8 6.28 us: shape_loops_on(): lax.dynamic_update_slice_in_dim(h_now, mixed_arr, (main - dev_j) % moved...]
    unnamed x103 -> x105, local copies, waits for them, and re-layouts: 23.1 us -> 23.1 us
  transfers between devices with their start and end apart: 10 -> 24, of which waited for: 7 -> 12; matrix products, arithmetic and copies ran while one was open for 16% -> 17% of each run, Pallas kernels for 0% -> 0%
where the time goes in v1:
time: 1040 us; the launch traced here: 1030 us
  waiting for transfers between devices  442 us (42%)
  matrix products  192 us (18%)
  blocking collectives  145 us (14%)
  other arithmetic  136 us (13%)
  local copies, waits for them, and re-layouts  66.3 us (6%)
  starting transfers between devices  32.2 us (3%)
  between operations  16.2 us (2%)
    unnamed x2, blocking collectives  125 us
    psum x1, waiting for transfers between devices, per_device(): mlp_sum = lax.psum(down_part.astype(jnp.bfloat16), 'mp').astype(jnp.float32)  115 us
    psum x1, waiting for transfers between devices, per_device(): lax.psum(jnp.einsum('psf,df->psd', d_pre, up_back, preferred_element_type...  82.4 us
    reduce_scatter x1, waiting for transfers between devices, per_device(): lax.psum_scatter(grad_w_down, 'dp', scatter_dimension=1, tiled=True)  79.2 us
    reduce_scatter x1, waiting for transfers between devices, per_device(): lax.psum_scatter(grad_w_qkv, 'dp', scatter_dimension=0, tiled=True)  71.9 us
    reduce_scatter x1, waiting for transfers between devices, per_device(): lax.psum_scatter(grad_w_up, 'dp', scatter_dimension=0, tiled=True)  54.5 us
    convert_element_type x1, other arithmetic, per_device(): active = jax.nn.gelu(pre_act, approximate=False).astype(low_type)  33.2 us
    ppermute x7, starting transfers between devices, shape_loops_on(): r2 = jax.lax.ppermute(r2, group_axis, perm=a_now)  30.7 us
  transfers between devices with their start and end apart: 24, of which 12 were waited for; matrix products, arithmetic and copies ran while one was open for 17% of the time, Pallas kernels for 0%

profile of v1, /device:TPU:0, one launch (start us, length us, event | category | flops | bytes accessed | tf_op | source)
XLA Modules:
  0.0 1029.6 jit_solution(835731046980263757)
XLA Ops:
  20.8 63.2 %all-reduce.13 = (bf16[768]{0:T(1024)(128)(2,1)}, bf16[768]{0:T(1024)(128)(2,1)}, bf16[768]{0:T(1024)(128)(2,1)}, bf16[768]{0:T(1024)(128)(2,1)}, bf16[768]{0:T(1024)(128)(2,1)}, /*index=5*/bf16[768]{0:T(1024)(128)(2,1)}) all-reduce(bf16[768]{0:T(1024)(128)(2,1)} %dynamic-update-slice.4, ...), channel_id=1, replica_groups=mesh['dp'=16,'mp'=2] {'dp'}, use_global_device_ids=true, to_apply=%add.4 | all-reduce | flops 4608 | bytes 18432
  97.2 20.3 %all_gather.30 = bf16[384,768]{0,1:T(8,128)(2,1)} all-gather(bf16[384,48]{0,1:T(8,128)(2,1)S(1)} %convert_element_type.183), channel_id=1, replica_groups=mesh['dp'=16,'mp'=2] {'dp'}, dimensions={1}, use_global_device_ids=true | all-gather | bytes 626688 | tf_op jit(solution)/shard_map/all_gather | solution.py:82
  117.5 7.1 fusion.96
  144.5 7.3 add_convert_fusion.3
  151.8 32.6 %while.22 = (s32[]{:T(128)}, bf16[4,2,280,6,64]{2,4,3,1,0:T(8,128)(2,1)}, f32[4,2,6,280]{3,2,1,0:T(8,128)S(1)}, bf16[4,2,280,6,64]{2,4,3,1,0:T(8,128)(2,1)}, f32...) while((s32[]{:T(128)}, ...), condition=%wide.region_5.6_spmd, body=%wide.region_2.5_spmd.sunk | while | flops 252346640 | bytes 13796445 | solution.py:138
  257.1 24.4 %all-reduce.19.cloned.1.call-done = bf16[8,280,768]{2,1,0:T(8,128)(2,1)} async-done(((bf16[8,280,768]{2,1,0:T(8,128)(2,1)}), bf16[8,280,768]{2,1,0:T(8,128)(2,1)}) %all-reduce.19.cloned.1.call-update) | async-done | bytes 3440656 | tf_op jit(solution)/shard_map/psum | solution.py:143
  287.4 12.6 %fusion.86 = (u8[280,1536]{1,0:T(8,128)(4,1)S(1)}, u8[280,1536]{1,0:T(8,128)(4,1)S(1)}, f32[8,280,1536]{2,1,0:T(8,128)S(1)}) fusion(f32[1536]{0:T(1024)S(1)} %copy-done.27, bf16[768,1536]{1,0:T(8,128)(2,1)} %constant_dynamic-update-slice_fusion, f32[768]{0:T(1024)S(1)} %copy-done.37, f32[768]{0:T(1024)S(1)} %copy-done.24, f32[8,280]{1,0:T(8,128)S(1)} %fusion.110, ...), kind=kOutput, calls=%fused_computation.134 | convolution fusion | flops 5347614720 | bytes 23896576 | tf_op jit(solution)/shard_map/psd,df->psf/dot_general | solution.py:147
  305.1 33.2 %multiply_convert_fusion.1 = (bf16[8,280,1536]{2,1,0:T(8,128)(2,1)}, f32[8,280,1536]{2,1,0:T(8,128)}) fusion(f32[8,280,1536]{2,1,0:T(8,128)S(1)} %get-tuple-element.189, f32[1536]{0:T(1024)S(1)} %copy-done.27, u8[280,1536]{1,0:T(8,128)(4,1)S(1)} %get-tuple-element.113, u8[280,1536]{1,0:T(8,128)(4,1)S(1)} %get-tuple-element.112), kind=kLoop, calls=%fused_computation.75 | loop fusion | flops 244285440 | bytes 35272704 | tf_op jit(solution)/shard_map/convert_element_type | solution.py:149
  338.3 18.4 %convert_reduce_fusion.1 = (f32[1536]{0:T(1024)}, bf16[8,280,1536]{2,1,0:T(8,128)(2,1)}) fusion(f32[8,280,1536]{2,1,0:T(8,128)} %get-tuple-element.173, bf16[1536,768]{0,1:T(8,128)(2,1)} %all-gather.5.cloned.1.call-done, bf16[8,280,768]{2,1,0:T(8,128)(2,1)} %param.21, f32[8,280]{1,0:T(8,128)} %fusion.108, f32[8,280,1536]{2,1,0:T(8,128)} %copy-done.6, ...), kind=kOutput, calls=%fused_computation.73 | convolution fusion | flops 5348473344 | bytes 40227584 | tf_op jit(solution)/shard_map/psd,fd->psf/dot_general | solution.py:161
  356.8 9.7 convolution_convert_fusion
  366.5 9.9 convolution_convert_fusion.1
  376.5 82.4 %all-reduce.21.cloned.1.call-done = bf16[8,280,768]{2,1,0:T(8,128)(2,1)} async-done(((bf16[8,280,768]{2,1,0:T(8,128)(2,1)}), bf16[8,280,768]{2,1,0:T(8,128)(2,1)}) %all-reduce.21.cloned.1.call-update) | async-done | bytes 3440656 | tf_op jit(solution)/shard_map/psum | solution.py:168
  485.6 63.8 %while.23 = (s32[]{:T(128)}, bf16[4,2,280,3,6,64]{2,5,4,1,3,0:T(8,128)(2,1)}, bf16[4,2,280,6,64]{2,4,3,1,0:T(8,128)(2,1)}, f32[4,2,280]{2,1,0:T(2,128)}, bf16[4,...) while((s32[]{:T(128)}, ...), condition=%wide.region_15.16_spmd, body=%wide.region_13.15_spmd.sunk | while | flops 621167104 | bytes 36805476 | solution.py:208
  556.6 7.7 bitcast_convert_fusion
  564.8 7.4 fusion.101
  572.3 12.6 %convolution_bitcast_fusion.1 = f32[768,1536]{1,0:T(8,128)} fusion(bf16[8,280,1536]{2,1,0:T(8,128)(2,1)} %get-tuple-element.191, f32[768]{0:T(1024)S(1)} %copy-done.38, f32[768]{0:T(1024)S(1)} %copy-done.26, f32[8,280]{1,0:T(8,128)S(1)} %copy-done.21, f32[8,280]{1,0:T(8,128)S(1)} %broadcast_multiply_fusion, f32[768]{0:T(1024)S(1)} %convert_element_type.187, ...), kind=kOutput, calls=%fused_computation.130 | convolution fusion | flops 5300305920 | bytes 18508288 | tf_op jit(solution)/shard_map/psd,psf->df/dot_general | solution.py:167
  584.9 11.0 %convolution_bitcast_fusion = f32[1536,768]{0,1:T(8,128)} fusion(bf16[8,280,1536]{2,1,0:T(8,128)(2,1)} %get-tuple-element.172, bf16[8,280,768]{2,1,0:T(8,128)(2,1)} %param.21, f32[8,280]{1,0:T(8,128)S(1)} %copy-done.18), kind=kOutput, calls=%fused_computation.129 | convolution fusion | flops 5289984000 | bytes 15049472 | tf_op jit(solution)/shard_map/psf,psd->fd/dot_general | solution.py:158
  596.2 13.8 %convolution_bitcast_fusion.2 = f32[768,3,384]{2,0,1:T(8,128)} fusion(bf16[8,280,3,384]{1,3,2,0:T(8,128)(2,1)} %bitcast.170, bf16[8,280,768]{2,1,0:T(8,128)(2,1)S(1)} %copy-done, f32[768]{0:T(1024)S(1)} %copy-done.36, f32[768]{0:T(1024)S(1)} %copy-done.23, f32[8,280]{1,0:T(8,128)S(1)} %copy-done.16, f32[8,280]{1,0:T(8,128)S(1)} %copy-done.11), kind=kOutput, calls=%fused_computation.144 | convolution fusion | flops 3973939200 | bytes 12164608 | tf_op jit(solution)/shard_map/psd,pstc->dtc/dot_general | solution.py:222
  615.1 115.3 %all-reduce.23.cloned.1.call-done = (bf16[8,280,768]{2,1,0:T(8,128)(2,1)}, bf16[8,280,768]{2,1,0:T(8,128)(2,1)}) async-done(((bf16[8,280,768]{2,1,0:T(8,128)(2,1)}, bf16[8,280,768]{2,1,0:T(8,128)(2,1)}), (bf16[8,280,768]{2,1,0:T(8,128)(2,1)}, bf16[8,280,768]{2,1,0:T(8,128)(2,1)})) %all-reduce.23.cloned.1.call-update) | async-done | bytes 6881296 | tf_op jit(solution)/shard_map/psum | solution.py:151
  739.0 61.8 %all-reduce.12 = (f32[768]{0:T(1024)S(1)}, f32[768]{0:T(1024)S(1)}, f32[2,384]{1,0:T(2,128)}, f32[768]{0:T(1024)}, f32[768]{0:T(1024)}, /*index=5*/f32[768]{0:T(1024)}, f32[1536]{0:T(1024)}, f32[768]{0:T(1024)S(1)}) all-reduce(f32[768]{0:T(1024)S(1)} %get-tuple-element.116, ...), channel_id=2, replica_groups=mesh['dp'=16,'mp'=2] {'dp'}, use_global_device_ids=true, to_apply=%region_20.21.clone | all-reduce | flops 6912 | bytes 55296
  806.4 11.0 %add_convert_fusion.1 = (bf16[8,280,768]{2,1,0:T(8,128)(2,1)}, bf16[8,280,768]{2,1,0:T(8,128)(2,1)}) fusion(f32[8,280,768]{2,1,0:T(8,128)} %copy-done.3, bf16[8,280,768]{2,1,0:T(8,128)(2,1)S(1)} %copy-done, bf16[8,280,768]{2,1,0:T(8,128)(2,1)} %get-tuple-element.169, f32[8,280]{1,0:T(8,128)S(1)} %negate_multiply_fusion.1, ...), kind=kLoop, calls=%fused_computation.116 | loop fusion | flops 32686080 | bytes 27579136 | tf_op jit(solution)/shard_map/convert_element_type | solution.py:230
  817.4 54.5 %reduce-scatter.9.cloned.1.call-done = f32[48,1536]{1,0:T(8,128)} async-done(((f32[768,1536]{1,0:T(8,128)}), f32[48,1536]{1,0:T(8,128)}) %reduce-scatter.9.cloned.1.call-update) | async-done | bytes 294928 | tf_op jit(solution)/shard_map/reduce_scatter | solution.py:235
  871.8 79.2 %reduce-scatter.11.cloned.1.call-done = f32[1536,48]{0,1:T(8,128)} async-done(((f32[1536,768]{0,1:T(8,128)}), f32[1536,48]{0,1:T(8,128)}) %reduce-scatter.11.cloned.1.call-update) | async-done | bytes 294928 | tf_op jit(solution)/shard_map/reduce_scatter | solution.py:236
  951.0 71.9 %reduce-scatter.5.cloned.1.call-done = f32[48,3,384]{2,0,1:T(8,128)} async-done(((f32[768,3,384]{2,0,1:T(8,128)}), f32[48,3,384]{2,0,1:T(8,128)}) %reduce-scatter.5.cloned.1.call-update) | async-done | bytes 221200 | tf_op jit(solution)/shard_map/reduce_scatter | solution.py:233
  (287 shorter events, 278.3 us)
Async XLA Ops:
  7.2 110.3 %all-gather.3.cloned.1.call-start = ((), (), s32[]{:S(2)}) async-start(), calls=%async_computation.4 | async-start | bytes 1880064 | tf_op jit(solution)/shard_map/all_gather | solution.py:81
  9.0 272.5 %all-reduce.19.cloned.1.call-start = ((), (), s32[]{:S(2)}) async-start(), calls=%async_computation.5 | async-start | bytes 6881280 | tf_op jit(solution)/shard_map/psum | solution.py:143
  190.4 147.9 %all-gather.5.cloned.1.call-start = ((), (), s32[]{:S(2)}) async-start(), calls=%async_computation.6 | async-start | bytes 2506752 | tf_op jit(solution)/shard_map/all_gather | solution.py:84
  193.7 10.9 %collective-permute-start = (bf16[48,1536]{1,0:T(8,128)(2,1)}, bf16[48,1536]{1,0:T(8,128)(2,1)}, u32[]{:S(2)}, u32[]{:S(2)}) collective-permute-start(bf16[48,1536]{1,0:T(8,128)(2,1)} %get-tuple-element.175), channel_id=1, source_target_pairs={{0,2},{2,4},{4,6},{6,8},{8,10},{10,12},{12,14},{14,16},{16,18},{18... | collective-permute-start | bytes 442376 | tf_op jit(solution)/shard_map/ppermute | solution.py:26
  194.1 10.5 %collective-permute-start.1 = (bf16[48,1536]{1,0:T(8,128)(2,1)}, bf16[48,1536]{1,0:T(8,128)(2,1)}, u32[]{:S(2)}, u32[]{:S(2)}) collective-permute-start(bf16[48,1536]{1,0:T(8,128)(2,1)} %get-tuple-element.175), channel_id=1, source_target_pairs={{0,30},{2,0},{4,2},{6,4},{8,6},{10,8},{12,10},{14,12},{16,14},{18,... | collective-permute-start | bytes 442376 | tf_op jit(solution)/shard_map/ppermute | solution.py:34
  199.8 259.0 %all-reduce.21.cloned.1.call-start = ((), (), s32[]{:S(2)}) async-start(), calls=%async_computation.7 | async-start | bytes 6881280 | tf_op jit(solution)/shard_map/psum | solution.py:168
  204.6 7.6 collective-permute-start.2
  204.6 7.6 collective-permute-start.3
  212.2 7.4 collective-permute-start.4
  212.2 7.4 collective-permute-start.5
  219.6 7.4 collective-permute-start.6
  219.6 7.4 collective-permute-start.7
  227.0 7.4 collective-permute-start.8
  227.0 7.4 collective-permute-start.9
  234.3 7.4 collective-permute-start.10
  234.3 7.4 collective-permute-start.11
  241.7 7.3 collective-permute-start.12
  241.7 8.1 collective-permute-start.13
  249.0 7.5 collective-permute-start.14
  366.5 364.0 %all-reduce.23.cloned.1.call-start = ((), (), s32[]{:S(2)}) async-start(), calls=%async_computation.12 | async-start | bytes 13762560 | tf_op jit(solution)/shard_map/psum | solution.py:151
  564.3 253.0 %reduce-scatter.7.cloned.1.call-start = ((), (), s32[]{:S(2)}) async-start(), calls=%async_computation.9 | async-start | bytes 1253376 | tf_op jit(solution)/shard_map/reduce_scatter | solution.py:234
  572.2 299.6 %reduce-scatter.9.cloned.1.call-start = ((), (), s32[]{:S(2)}) async-start(), calls=%async_computation.10 | async-start | bytes 5013504 | tf_op jit(solution)/shard_map/reduce_scatter | solution.py:235
  584.9 366.1 %reduce-scatter.11.cloned.1.call-start = ((), (), s32[]{:S(2)}) async-start(), calls=%async_computation.11 | async-start | bytes 5013504 | tf_op jit(solution)/shard_map/reduce_scatter | solution.py:236
  595.9 427.0 %reduce-scatter.5.cloned.1.call-start = ((), (), s32[]{:S(2)}) async-start(), calls=%async_computation.8 | async-start | bytes 3760128 | tf_op jit(solution)/shard_map/reduce_scatter | solution.py:233
  (43 other events, 600.6 us)
Sparse Core Ops, SparseCore 0:
  10.9 43.1 all-gather.2
  190.6 90.9 all-reduce.18
  284.4 42.3 all-gather.4
  366.6 92.2 all-reduce.20
  564.4 165.9 all-reduce.22
  734.5 58.2 reduce-scatter.6
  797.2 74.6 reduce-scatter.8
  876.3 74.7 reduce-scatter.10
  955.5 67.3 reduce-scatter.4
